TPU v7x, 256 devices: a whole 4x4x8 slice. The times are simulated.
256 devices in a mesh: dp: 16 (over y, z_hi), mp: 16 (over x, z_lo, core).
Axes of the slice: x: 4, y: 4, z: 8 (z_hi: 4, z_lo: 2; z = z_hi * 2 + z_lo), core: 2. Of those that a mesh axis runs over, the one named last changes fastest.
Arguments:
- inputs: bfloat16 [16, 512, 4096], P('dp', None, 'mp'), may hold values from -6 to 6
- out_grads: bfloat16 [16, 512, 4096], P('dp', None, 'mp'), may hold values from -6 to 6
- gate_weight: bfloat16 [4096, 14336], P('dp', 'mp'), may hold values from -0.09375 to 0.09375
- down_weight: bfloat16 [14336, 4096], P('mp', 'dp'), may hold values from -0.046875 to 0.046875
- in_proj: bfloat16 [4096, 64], replicated, may hold values from -0.09375 to 0.09375
- out_proj: bfloat16 [14336, 64], P('mp'), may hold values from -0.046875 to 0.046875
- in_precond: float32 [64, 64], replicated, may hold values from -0.75 to 0.75
- out_precond: float32 [64, 64], replicated, may hold values from -0.75 to 0.75
- queries: bfloat16 [2048, 4096], P('dp', 'mp'), may hold values from -48 to 48
- languages: int32 [2048], P('dp'), may hold values from 0 to 31, as said below
Outputs:
- influence: float32 [16, 32], P('dp')
Inputs may be any that keep to these rules, and one draw needn't show every extreme that they name: Each of the 32 languages labels exactly 64 queries.
All inputs are finite; a program needn't handle non-finite values.
Results may differ from a plain program's by a relative error of at most 0.0042.
Values may be sent and summed in bfloat16 or wider, within the bound.
No kernel may reach another device: no remote copies, remote signals or barrier semaphores. Data moves between devices by JAX's collectives and lax.ppermute only.
A program may use at most 128 MiB of HBM per device.

v0:
```python
import jax
import jax.numpy as jnp
from jax import lax
from jax.sharding import PartitionSpec as P

LANGS = 32


def shards(
    inputs,
    out_grads,
    gate_weight,
    down_weight,
    in_proj,
    out_proj,
    in_precond,
    out_precond,
    queries,
    languages,
):
    examples = inputs.shape[0]
    seq_len = inputs.shape[1]
    rows_full, grads_full = (
        lax.all_gather(inputs, "mp", axis=2, tiled=True),
        lax.all_gather(out_grads, "mp", axis=2, tiled=True),
    )
    tok_rows = rows_full.reshape(examples * seq_len, rows_full.shape[2])
    tok_grads = grads_full.reshape(examples * seq_len, grads_full.shape[2])
    columns = tok_rows
    gate = jnp.dot(
        columns,
        lax.all_gather(gate_weight, "dp", axis=0, tiled=True),
        preferred_element_type=jnp.float32,
    )
    columns = tok_grads
    hidden_grad = lax.dot_general(
        columns,
        lax.all_gather(down_weight, "dp", axis=1, tiled=True),
        (((1,), (1,)), ((), ())),
        preferred_element_type=jnp.float32,
    )
    up_grad = (hidden_grad * jax.nn.silu(gate)).astype(jnp.bfloat16)
    rank = in_proj.shape[1]
    band = rank // lax.axis_size("mp")
    in_factor = jnp.dot(
        jnp.dot(tok_rows, in_proj, preferred_element_type=jnp.float32),
        in_precond.T,
        precision=lax.Precision.HIGHEST,
    )
    in_three = in_factor.reshape(examples, seq_len, rank)
    out_part = jnp.dot(up_grad, out_proj, preferred_element_type=jnp.float32)
    out_sum = lax.psum(out_part, "mp")
    out_factor = jnp.dot(out_sum, out_precond, precision=lax.Precision.HIGHEST)
    full = (
        jnp.einsum(
            "esi,esj->eij",
            in_three,
            out_factor.reshape(examples, seq_len, rank),
            precision=lax.Precision.HIGHEST,
        )
        / seq_len
    )
    own_block = lax.dynamic_slice_in_dim(full, lax.axis_index("mp") * band, band, 1)
    projected = own_block.reshape(examples, band * rank).astype(jnp.bfloat16)
    per_language = languages.shape[0] * lax.axis_size("dp") // LANGS
    lang_ids = jnp.arange(LANGS, dtype=jnp.int32)
    query_piece = lax.all_gather(queries, "dp", axis=0, tiled=True)
    label_piece = lax.all_gather(languages, "dp", axis=0, tiled=True)
    block_scores = lax.dot_general(
        projected, query_piece, (((1,), (1,)), ((), ())), preferred_element_type=jnp.float32
    )
    onehot = (label_piece[:, None] == lang_ids[None, :]).astype(jnp.float32)
    partial_sums = jnp.dot(block_scores, onehot, precision=lax.Precision.HIGHEST)
    totals = lax.psum(partial_sums, "mp")
    return totals / per_language


def solution(mesh):
    return jax.shard_map(
        shards,
        mesh=mesh,
        in_specs=(
            P("dp", None, "mp"),
            P("dp", None, "mp"),
            P("dp", "mp"),
            P("mp", "dp"),
            P(),
            P("mp", None),
            P(),
            P(),
            P("dp", "mp"),
            P("dp"),
        ),
        out_specs=P("dp", None),
        check_vma=False,
    )
```

profile of v0, /device:TPU:1, one launch (start us, length us, event | category | flops | bytes accessed | tf_op | source)
XLA Modules:
  0.0 558.4 jit_solution(12647882360686652842)
XLA Ops:
  6.5 0.7 all-gather.7.cloned.1.call-update
  7.3 0.7 all-gather.13.cloned.1.call-update
  8.1 0.7 all-gather.9.cloned.1.call-update
  8.8 0.5 all-gather.11.cloned.1.call-update
  9.4 52.4 %all-gather.7.cloned.1.call-done = bf16[1,512,4096]{2,1,0:T(8,128)(2,1)} async-done(((bf16[1,512,256]{2,1,0:T(8,128)(2,1)}), bf16[1,512,4096]{2,1,0:T(8,128)(2,1)}) %all-gather.7.cloned.1.call-update) | async-done | bytes 4194320 | tf_op jit(solution)/shard_map/all_gather | solution.py:24
  61.8 96.9 %all-gather.13.cloned.1.call-done = bf16[4096,896]{1,0:T(8,128)(2,1)} async-done(((bf16[256,896]{1,0:T(8,128)(2,1)}), bf16[4096,896]{1,0:T(8,128)(2,1)}) %all-gather.13.cloned.1.call-update) | async-done | bytes 7340048 | tf_op jit(solution)/shard_map/all_gather | solution.py:32
  158.7 10.1 %fusion.2 = f32[512,896]{1,0:T(8,128)S(1)} fusion(bf16[4096,896]{1,0:T(8,128)(2,1)} %all-gather.13.cloned.1.call-done, bf16[1,512,4096]{2,1,0:T(8,128)(2,1)} %all-gather.7.cloned.1.call-done), kind=kOutput, calls=%fused_computation.2 | convolution fusion | flops 3758096384 | bytes 13369344 | tf_op jit(solution)/shard_map/dot_general | solution.py:30
  168.8 50.9 %all-gather.9.cloned.1.call-done = bf16[1,512,4096]{2,1,0:T(8,128)(2,1)} async-done(((bf16[1,512,256]{2,1,0:T(8,128)(2,1)}), bf16[1,512,4096]{2,1,0:T(8,128)(2,1)}) %all-gather.9.cloned.1.call-update) | async-done | bytes 4194320 | tf_op jit(solution)/shard_map/all_gather | solution.py:25
  219.7 115.6 %all-gather.11.cloned.1.call-done = bf16[896,4096]{1,0:T(8,128)(2,1)} async-done(((bf16[896,256]{1,0:T(8,128)(2,1)}), bf16[896,4096]{1,0:T(8,128)(2,1)}) %all-gather.11.cloned.1.call-update) | async-done | bytes 7340048 | tf_op jit(solution)/shard_map/all_gather | solution.py:38
  335.3 9.9 %fusion.9 = f32[512,64]{1,0:T(8,128)} fusion(bf16[896,64]{0,1:T(8,128)(2,1)S(1)} %copy-done.4, f32[512,896]{1,0:T(8,128)S(1)} %fusion.2, bf16[896,4096]{1,0:T(8,128)(2,1)} %all-gather.11.cloned.1.call-done, bf16[1,512,4096]{2,1,0:T(8,128)(2,1)} %all-gather.9.cloned.1.call-done), kind=kOutput, calls=%fused_computation.8 | convolution fusion | flops 3819569152 | bytes 13615104 | tf_op jit(solution)/shard_map/dot_general | solution.py:51
  345.3 0.0 all-gather.15.cloned.1.call-start
  345.3 0.5 all-gather.15.cloned.1.call-update
  345.9 34.9 %all-gather = s32[16,1,128]{2,1,0:T(1,128)S(1)} all-gather(s32[1,1,128]{2,1,0:T(1,128)S(1)} %bitcast.32), channel_id=1, replica_groups=mesh['dp'=16,'mp'=16] {'dp'}, dimensions={0}, use_global_device_ids=true | all-gather | bytes 8704 | tf_op jit(solution)/shard_map/all_gather | solution.py:68
  380.7 3.4 fusion.4
  384.2 0.4 fusion.16
  384.5 80.6 %all-reduce.2.cloned.1.call-done = f32[512,64]{1,0:T(8,128)} async-done(((f32[512,64]{1,0:T(8,128)}), f32[512,64]{1,0:T(8,128)}) %all-reduce.2.cloned.1.call-update) | async-done | bytes 131088 | tf_op jit(solution)/shard_map/psum | solution.py:52
  465.1 1.3 fusion.17
  466.4 0.6 fusion.18
  467.1 0.1 reshape.32
  467.1 53.2 %all-gather.15.cloned.1.call-done = bf16[2048,256]{1,0:T(8,128)(2,1)} async-done(((bf16[128,256]{1,0:T(8,128)(2,1)}), bf16[2048,256]{1,0:T(8,128)(2,1)}) %all-gather.15.cloned.1.call-update) | async-done | bytes 1048592 | tf_op jit(solution)/shard_map/all_gather | solution.py:67
  520.4 1.6 convolution_bitcast_fusion
  522.0 0.6 fusion.11
  522.5 28.5 %psum.15 = f32[1,32]{1,0:T(1,128)S(1)} all-reduce(f32[1,32]{1,0:T(1,128)S(1)} %fusion.11), channel_id=1, replica_groups=mesh['dp'=16,'mp'=16] {'mp'}, use_global_device_ids=true, to_apply=%region_1.2 | all-reduce | flops 32 | bytes 256 | tf_op jit(solution)/shard_map/psum | solution.py:74
  551.0 0.5 broadcast_multiply_fusion
  (17 shorter events, 0.2 us)
Async XLA Ops:
  6.5 374.2 %copy-start = (bf16[4096,64]{0,1:T(8,128)(2,1)S(1)}, bf16[4096,64]{0,1:T(8,128)(2,1)}, u32[]{:S(2)}) copy-start(bf16[4096,64]{0,1:T(8,128)(2,1)} %param.14) | copy-start | bytes 1572868
  6.5 55.3 %all-gather.7.cloned.1.call-start = ((), (), s32[]{:S(2)}) async-start(), calls=%async_computation | async-start | bytes 4456448 | tf_op jit(solution)/shard_map/all_gather | solution.py:24
  7.3 151.4 %all-gather.13.cloned.1.call-start = ((), (), s32[]{:S(2)}) async-start(), calls=%async_computation.3 | async-start | bytes 7798784 | tf_op jit(solution)/shard_map/all_gather | solution.py:32
  8.0 211.7 %all-gather.9.cloned.1.call-start = ((), (), s32[]{:S(2)}) async-start(), calls=%async_computation.1 | async-start | bytes 4456448 | tf_op jit(solution)/shard_map/all_gather | solution.py:25
  8.7 326.6 %all-gather.11.cloned.1.call-start = ((), (), s32[]{:S(2)}) async-start(), calls=%async_computation.2 | async-start | bytes 7798784 | tf_op jit(solution)/shard_map/all_gather | solution.py:38
  9.3 326.0 %copy-start.4 = (bf16[896,64]{0,1:T(8,128)(2,1)S(1)}, bf16[896,64]{0,1:T(8,128)(2,1)}, u32[]{:S(2)}) copy-start(bf16[896,64]{0,1:T(8,128)(2,1)} %param.15) | copy-start | bytes 344068
  9.3 455.8 %all-reduce.2.cloned.1.call-start = ((), (), s32[]{:S(2)}) async-start(), calls=%async_computation.4 | async-start | bytes 524288 | tf_op jit(solution)/shard_map/psum | solution.py:52
  168.8 177.1 %copy-start.3 = (s32[128]{0:T(128)S(1)}, s32[128]{0:T(128)}, u32[]{:S(2)}) copy-start(s32[128]{0:T(128)} %param.19) | copy-start | bytes 1540
  345.2 38.9 %copy-start.1 = (f32[64,64]{1,0:T(8,128)S(1)}, f32[64,64]{1,0:T(8,128)}, u32[]{:S(2)}) copy-start(f32[64,64]{1,0:T(8,128)} %param.16) | copy-start | bytes 49156
  345.2 119.9 %copy-start.2 = (f32[64,64]{1,0:T(8,128)S(1)}, f32[64,64]{1,0:T(8,128)}, u32[]{:S(2)}) copy-start(f32[64,64]{1,0:T(8,128)} %param.17) | copy-start | bytes 49156
  345.3 175.1 %all-gather.15.cloned.1.call-start = ((), (), s32[]{:S(2)}) async-start(), calls=%async_computation.5 | async-start | bytes 1114112 | tf_op jit(solution)/shard_map/all_gather | solution.py:67
Sparse Core Ops, SparseCore 0:
  9.1 52.6 all-gather.6
  64.3 94.3 all-gather.12
  160.5 59.2 all-gather.8
  222.0 113.2 all-gather.10
  345.4 119.6 all-reduce.1
  467.7 52.6 all-gather.14
where the time goes:
time: 559 us; the launch traced here: 558 us
  waiting for transfers between devices  453 us (81%)
  blocking collectives  63.3 us (11%)
  matrix products  27.9 us (5%)
  between operations  13.6 us (2%)
    all_gather x1, waiting for transfers between devices, shards(): lax.all_gather(down_weight, 'dp', axis=1, tiled=True)  116 us
    all_gather x1, waiting for transfers between devices, shards(): lax.all_gather(gate_weight, 'dp', axis=0, tiled=True)  96.9 us
    psum x1, waiting for transfers between devices, shards(): out_sum = lax.psum(out_part, 'mp')  80.6 us
    all_gather x1, waiting for transfers between devices, shards(): query_piece = lax.all_gather(queries, 'dp', axis=0, tiled=True)  53.2 us
    all_gather x1, waiting for transfers between devices, shards(): lax.all_gather(inputs, 'mp', axis=2, tiled=True)  52.4 us
    all_gather x1, waiting for transfers between devices, shards(): lax.all_gather(out_grads, 'mp', axis=2, tiled=True)  50.9 us
    all_gather x1, blocking collectives, shards(): label_piece = lax.all_gather(languages, 'dp', axis=0, tiled=True)  34.9 us
    psum x1, blocking collectives, shards(): totals = lax.psum(partial_sums, 'mp')  28.5 us
  transfers between devices with their start and end apart: 6, of which 6 were waited for; matrix products, arithmetic and copies ran while one was open for 3% of the time, Pallas kernels for 0%

commit v1 on v0

--- a/solution.py
+++ b/solution.py
@@ -49,7 +49,7 @@
     )
     in_three = in_factor.reshape(examples, seq_len, rank)
     out_part = jnp.dot(up_grad, out_proj, preferred_element_type=jnp.float32)
-    out_sum = lax.psum(out_part, "mp")
+    out_sum = jnp.sum(lax.all_gather(out_part, "mp"), axis=0)
     out_factor = jnp.dot(out_sum, out_precond, precision=lax.Precision.HIGHEST)
     full = (
         jnp.einsum(

time: 559 us -> 473 us (0.85)
  waiting for transfers between devices: 453 us -> 365 us
    psum x1 -> x0, waiting for transfers between devices: 80.6 us -> none  [shards(): out_sum = lax.psum(out_part, 'mp')]
    all_gather x1, waiting for transfers between devices: 53.2 us -> 46 us  [shards(): query_piece = lax.all_gather(queries, 'dp', axis=0, tiled=True)]
  transfers between devices with their start and end apart: 6 -> 6, of which waited for: 6 -> 5; matrix products, arithmetic and copies ran while one was open for 3% -> 4% of each run, Pallas kernels for 0% -> 0%
where the time goes in v1:
time: 473 us
  waiting for transfers between devices  365 us (77%)
  blocking collectives  63.5 us (13%)
  matrix products  27.1 us (6%)
  between operations  13.6 us (3%)
    all_gather x1, waiting for transfers between devices, shards(): lax.all_gather(down_weight, 'dp', axis=1, tiled=True)  116 us
    all_gather x1, waiting for transfers between devices, shards(): lax.all_gather(gate_weight, 'dp', axis=0, tiled=True)  96.9 us
    all_gather x1, waiting for transfers between devices, shards(): lax.all_gather(inputs, 'mp', axis=2, tiled=True)  52.4 us
    all_gather x1, waiting for transfers between devices, shards(): lax.all_gather(out_grads, 'mp', axis=2, tiled=True)  50.9 us
    all_gather x1, waiting for transfers between devices, shards(): query_piece = lax.all_gather(queries, 'dp', axis=0, tiled=True)  46 us
    all_gather x1, blocking collectives, shards(): label_piece = lax.all_gather(languages, 'dp', axis=0, tiled=True)  35.1 us
    psum x1, blocking collectives, shards(): totals = lax.psum(partial_sums, 'mp')  28.5 us
    dot_general x1, matrix products, shards(): jnp.dot(columns, lax.all_gather(gate_weight, 'dp', axis=0, tiled=True), p...  10.1 us
  transfers between devices with their start and end apart: 6, of which 5 were waited for; matrix products, arithmetic and copies ran while one was open for 4% of the time, Pallas kernels for 0%

profile of v1, /device:TPU:1, one launch (start us, length us, event | category | flops | bytes accessed | tf_op | source)
XLA Modules:
  0.0 473.2 jit_solution(2856740098953321362)
XLA Ops:
  6.5 0.7 all-gather.9.cloned.1.call-update
  7.3 0.7 all-gather.15.cloned.1.call-update
  8.1 0.7 all-gather.11.cloned.1.call-update
  8.8 0.5 all-gather.13.cloned.1.call-update
  9.4 52.4 %all-gather.9.cloned.1.call-done = bf16[1,512,4096]{2,1,0:T(8,128)(2,1)} async-done(((bf16[1,512,256]{2,1,0:T(8,128)(2,1)}), bf16[1,512,4096]{2,1,0:T(8,128)(2,1)}) %all-gather.9.cloned.1.call-update) | async-done | bytes 4194320 | tf_op jit(solution)/shard_map/all_gather | solution.py:24
  61.8 96.9 %all-gather.15.cloned.1.call-done = bf16[4096,896]{1,0:T(8,128)(2,1)} async-done(((bf16[256,896]{1,0:T(8,128)(2,1)}), bf16[4096,896]{1,0:T(8,128)(2,1)}) %all-gather.15.cloned.1.call-update) | async-done | bytes 7340048 | tf_op jit(solution)/shard_map/all_gather | solution.py:32
  158.7 10.1 %fusion.2 = f32[512,896]{1,0:T(8,128)S(1)} fusion(bf16[4096,896]{1,0:T(8,128)(2,1)} %all-gather.15.cloned.1.call-done, bf16[1,512,4096]{2,1,0:T(8,128)(2,1)} %all-gather.9.cloned.1.call-done), kind=kOutput, calls=%fused_computation.2 | convolution fusion | flops 3758096384 | bytes 13369344 | tf_op jit(solution)/shard_map/dot_general | solution.py:30
  168.8 50.9 %all-gather.11.cloned.1.call-done = bf16[1,512,4096]{2,1,0:T(8,128)(2,1)} async-done(((bf16[1,512,256]{2,1,0:T(8,128)(2,1)}), bf16[1,512,4096]{2,1,0:T(8,128)(2,1)}) %all-gather.11.cloned.1.call-update) | async-done | bytes 4194320 | tf_op jit(solution)/shard_map/all_gather | solution.py:25
  219.7 115.6 %all-gather.13.cloned.1.call-done = bf16[896,4096]{1,0:T(8,128)(2,1)} async-done(((bf16[896,256]{1,0:T(8,128)(2,1)}), bf16[896,4096]{1,0:T(8,128)(2,1)}) %all-gather.13.cloned.1.call-update) | async-done | bytes 7340048 | tf_op jit(solution)/shard_map/all_gather | solution.py:38
  335.3 9.9 %fusion.9 = f32[512,64]{0,1:T(8,128)} fusion(bf16[896,64]{0,1:T(8,128)(2,1)S(1)} %copy-done.4, f32[512,896]{1,0:T(8,128)S(1)} %fusion.2, bf16[896,4096]{1,0:T(8,128)(2,1)} %all-gather.13.cloned.1.call-done, bf16[1,512,4096]{2,1,0:T(8,128)(2,1)} %all-gather.11.cloned.1.call-done), kind=kOutput, calls=%fused_computation.9 | convolution fusion | flops 3819569152 | bytes 13615104 | tf_op jit(solution)/shard_map/dot_general | solution.py:51
  345.2 0.5 all-gather.17.cloned.1.call-update
  345.8 35.1 %all-gather.1 = s32[16,1,128]{2,1,0:T(1,128)S(1)} all-gather(s32[1,1,128]{2,1,0:T(1,128)S(1)} %bitcast.38), channel_id=1, replica_groups=mesh['dp'=16,'mp'=16] {'dp'}, dimensions={0}, use_global_device_ids=true | all-gather | bytes 8704 | tf_op jit(solution)/shard_map/all_gather | solution.py:68
  380.9 3.4 fusion.4
  384.3 0.4 fusion.16
  384.7 2.8 copy.11
  387.5 0.3 bitcast_reduce_fusion
  387.9 0.6 fusion.17
  388.5 0.6 fusion.18
  389.1 0.1 reshape.33
  389.2 46.0 %all-gather.17.cloned.1.call-done = bf16[2048,256]{1,0:T(8,128)(2,1)} async-done(((bf16[128,256]{1,0:T(8,128)(2,1)}), bf16[2048,256]{1,0:T(8,128)(2,1)}) %all-gather.17.cloned.1.call-update) | async-done | bytes 1048592 | tf_op jit(solution)/shard_map/all_gather | solution.py:67
  435.1 1.6 convolution_bitcast_fusion
  436.7 0.6 fusion.11
  437.3 28.5 %psum.7 = f32[1,32]{1,0:T(1,128)S(1)} all-reduce(f32[1,32]{1,0:T(1,128)S(1)} %fusion.11), channel_id=1, replica_groups=mesh['dp'=16,'mp'=16] {'mp'}, use_global_device_ids=true, to_apply=%region_1.2 | all-reduce | flops 32 | bytes 256 | tf_op jit(solution)/shard_map/psum | solution.py:74
  465.8 0.5 broadcast_multiply_fusion
  (19 shorter events, 0.3 us)
Async XLA Ops:
  6.5 374.3 %copy-start = (bf16[4096,64]{0,1:T(8,128)(2,1)S(1)}, bf16[4096,64]{0,1:T(8,128)(2,1)}, u32[]{:S(2)}) copy-start(bf16[4096,64]{0,1:T(8,128)(2,1)} %param.14) | copy-start | bytes 1572868
  6.5 55.3 %all-gather.9.cloned.1.call-start = ((), (), s32[]{:S(2)}) async-start(), calls=%async_computation | async-start | bytes 4456448 | tf_op jit(solution)/shard_map/all_gather | solution.py:24
  7.3 151.4 %all-gather.15.cloned.1.call-start = ((), (), s32[]{:S(2)}) async-start(), calls=%async_computation.3 | async-start | bytes 7798784 | tf_op jit(solution)/shard_map/all_gather | solution.py:32
  8.0 211.7 %all-gather.11.cloned.1.call-start = ((), (), s32[]{:S(2)}) async-start(), calls=%async_computation.1 | async-start | bytes 4456448 | tf_op jit(solution)/shard_map/all_gather | solution.py:25
  8.7 326.6 %all-gather.13.cloned.1.call-start = ((), (), s32[]{:S(2)}) async-start(), calls=%async_computation.2 | async-start | bytes 7798784 | tf_op jit(solution)/shard_map/all_gather | solution.py:38
  9.3 326.0 %copy-start.4 = (bf16[896,64]{0,1:T(8,128)(2,1)S(1)}, bf16[896,64]{0,1:T(8,128)(2,1)}, u32[]{:S(2)}) copy-start(bf16[896,64]{0,1:T(8,128)(2,1)} %param.15) | copy-start | bytes 344068
  9.3 375.4 %all-gather.19.cloned.1.call-start = ((), (), s32[]{:S(2)}) async-start(), calls=%async_computation.5 | async-start | bytes 2228224 | tf_op jit(solution)/shard_map/all_gather | solution.py:52
  168.8 177.0 %copy-start.3 = (s32[128]{0:T(128)S(1)}, s32[128]{0:T(128)}, u32[]{:S(2)}) copy-start(s32[128]{0:T(128)} %param.19) | copy-start | bytes 1540
  345.2 39.1 %copy-start.1 = (f32[64,64]{1,0:T(8,128)S(1)}, f32[64,64]{1,0:T(8,128)}, u32[]{:S(2)}) copy-start(f32[64,64]{1,0:T(8,128)} %param.16) | copy-start | bytes 49156
  345.2 89.9 %all-gather.17.cloned.1.call-start = ((), (), s32[]{:S(2)}) async-start(), calls=%async_computation.4 | async-start | bytes 1114112 | tf_op jit(solution)/shard_map/all_gather | solution.py:67
  384.3 3.6 copy-start.2
Sparse Core Ops, SparseCore 0:
  9.1 52.6 all-gather.8
  64.3 94.3 all-gather.14
  160.5 59.2 all-gather.10
  222.0 113.2 all-gather.12
  345.3 35.4 all-gather.18
  383.1 52.0 all-gather.16
